TPU v7x, 256 devices: a whole 4x4x8 slice. The times are simulated.
256 devices in a mesh: tm: 8 (over x, core), row: 32 (over z, y).
Axes of the slice: x: 4, y: 4, z: 8, core: 2. Of those that a mesh axis runs over, the one named last changes fastest.
Arguments:
- pred_cov: bfloat16 [8, 1536, 1536], P('tm', 'row'), may hold values from -0.8 to 3.3, as said below
- cross: float32 [8, 1536, 1536], P('tm', 'row'), may hold values from -0.9 to 3.2
- filt_mean: float32 [8, 1536], P('tm', 'row'), may hold values from -6 to 6
- pred_mean: float32 [8, 1536], P('tm', 'row'), may hold values from -6 to 6
- next_smoothed: float32 [1536], P('row'), may hold values from -6 to 6
Outputs:
- smoothed: float32 [8, 1536], P('tm', 'row')
- gains: float32 [8, 1536, 1536], P('tm', 'row')
Inputs may be any that keep to these rules, and one draw needn't show every extreme that they name: `pred_cov`: each of the 8 matrices of size 1536 x 1536 is symmetric positive definite.
All inputs are finite; a program needn't handle non-finite values.
Results may differ from a plain program's by a relative error of at most 0.0003.
Values may be sent and summed in bfloat16 or wider, within the bound.
No kernel may reach another device: no remote copies, remote signals or barrier semaphores. Data moves between devices by JAX's collectives and lax.ppermute only.
A program may use at most 128 MiB of HBM per device.

v0:
```python
import jax
import jax.numpy as jnp
from jax import lax
from jax.sharding import PartitionSpec as P

finest = lax.Precision.HIGHEST


def from_behind(array, axis, by):
    peers = lax.axis_size(axis)
    pairs = [(i, i + by) for i in range(peers) if 0 <= i + by < peers]
    return lax.ppermute(array, axis, pairs)


def matvec(matrix, vector):
    return jnp.dot(matrix, vector, precision=finest, preferred_element_type=jnp.float32)


def per_device(pred_cov, cross, filt_mean, pred_mean, next_smoothed):
    whole_cov = lax.all_gather(pred_cov, "row", axis=1, tiled=True)
    cholesky_factor = jnp.linalg.cholesky(whole_cov[0].astype(jnp.float32))
    gain = jax.scipy.linalg.cho_solve((cholesky_factor, True), cross[0].T).T
    steps = lax.axis_size("tm")
    final = lax.axis_index("tm") == steps - 1
    mean_f = filt_mean[0]
    mean_p = pred_mean[0]

    def advance(turn, state):
        later = from_behind(state, "tm", -1)
        later = jnp.where(final, next_smoothed, later)
        dispersion = lax.all_gather(later - mean_p, "row", axis=0, tiled=True)
        return mean_f + matvec(gain, dispersion)

    smoothed = lax.fori_loop(0, steps, advance, jnp.zeros_like(mean_f))
    return (smoothed[None, :], gain[None, :, :])


def solution(mesh):
    in_specs = (
        P("tm", "row", None),
        P("tm", "row", None),
        P("tm", "row"),
        P("tm", "row"),
        P("row"),
    )
    out_specs = (P("tm", "row"), P("tm", "row", None))
    return jax.shard_map(
        per_device, mesh=mesh, in_specs=in_specs, out_specs=out_specs, check_vma=False
    )
```

profile of v0, /device:TPU:12, one launch (start us, length us, event | category | flops | bytes accessed | tf_op | source)
XLA Modules:
  0.0 1279.2 jit_solution(8773022271125293121)
XLA Ops:
  7.9 87.8 %all-gather.2.cloned.1.call-done = bf16[1,1536,1536]{2,1,0:T(8,128)(2,1)} async-done(((bf16[1,48,1536]{2,1,0:T(8,128)(2,1)}), bf16[1,1536,1536]{2,1,0:T(8,128)(2,1)}) %all-gather.2.cloned.1.call-update) | async-done | bytes 4718608 | tf_op jit(solution)/shard_map/all_gather | solution.py:20
  95.8 6.6 copy.9
  102.4 7.3 bitcast_convert_fusion
  109.7 9.6 copy.10
  119.4 6.5 fusion.3
  125.9 3.6 copy-done
  129.5 11.7 cholesky.341
  141.3 9.8 custom-call.98
  151.1 4.8 cholesky.371
  155.9 2.8 constant_dynamic-update-slice_fusion.134
  160.6 12.0 cholesky.362
  173.3 9.8 custom-call.99
  184.7 2.8 convolution_subtract_fusion.1
  187.4 11.7 cholesky.385
  200.5 9.8 custom-call.100
  211.9 3.3 convolution_subtract_fusion
  215.3 11.7 cholesky.715
  228.3 9.8 custom-call.101
  239.6 3.6 fusion.20
  243.1 11.9 cholesky.734
  256.3 9.8 custom-call.102
  267.5 3.8 fusion.23
  271.4 11.7 cholesky.754
  284.3 10.2 custom-call.103
  295.8 3.8 fusion.26
  299.6 11.7 cholesky.774
  312.7 9.8 custom-call.104
  323.7 3.8 fusion.29
  327.5 11.9 cholesky.794
  340.7 9.8 custom-call.105
  351.6 3.6 fusion.32
  355.2 11.7 cholesky.814
  368.3 10.2 custom-call.106
  379.5 3.3 fusion.35
  382.8 11.7 cholesky.834
  395.7 9.8 custom-call.107
  406.5 2.8 fusion.38
  409.3 11.9 cholesky.854
  422.5 9.8 custom-call.108
  435.5 11.7 cholesky.872
  456.7 8.5 select_select_fusion
  465.2 42.9 %while.12 = (s32[]{:T(128)}, f32[1536,1536]{1,0:T(8,128)}, s32[12,2]{0,1:T(2,128)S(1)}, f32[12,128,128]{2,1,0:T(8,128)}, s32[]{:T(128)}) while((s32[]{:T(128)}, f32[1536,1536]{1,0:T(8,128)}, s32[12,2]{0,1:T(2,128)S(1)}, f32[12,128,128]{2,1,0:T(8,128)}, s32[]{:T(128)}) %tuple.127), condition=%wide.while_cond, body=%wide.while_body.sunk | while | flops 2 | bytes 132705 | solution.py:22
  465.9 2.9 bitcast_dynamic-update-slice_fusion.2
  469.5 2.9 bitcast_dynamic-update-slice_fusion.2
  473.1 2.9 bitcast_dynamic-update-slice_fusion.2
  476.7 2.9 bitcast_dynamic-update-slice_fusion.2
  480.2 2.9 bitcast_dynamic-update-slice_fusion.2
  483.8 2.9 bitcast_dynamic-update-slice_fusion.2
  487.4 2.9 bitcast_dynamic-update-slice_fusion.2
  491.0 2.9 bitcast_dynamic-update-slice_fusion.2
  494.6 2.9 bitcast_dynamic-update-slice_fusion.2
  498.1 2.9 bitcast_dynamic-update-slice_fusion.2
  501.7 2.9 bitcast_dynamic-update-slice_fusion.2
  505.3 2.8 bitcast_dynamic-update-slice_fusion.2
  508.2 118.9 %custom-call.109 = f32[12,128,128]{1,2,0:T(8,128)S(1)} custom-call(f32[12,128,128]{2,1,0:T(8,128)} %get-tuple-element.47), custom_call_target="InvertDiagBlocksLowerTriangular" | custom-call | tf_op jit(solution)/shard_map/jit(_cho_solve)/triangular_solve | solution.py:22
  664.9 606.3 %while.13 = (s32[]{:T(128)}, f32[48]{0:T(128)S(1)}, pred[]{:T(512)}, f32[48]{0:T(128)S(1)}, f32[48]{0:T(128)S(1)}, /*index=5*/f32[48,1536]{1,0:T(8,128)S(1)}, f3...) while((s32[]{:T(128)}, f32[48]{0:T(128)S(1)}, ...), condition=%wide.region_25.26_spmd.clone, body=%wide.region_24.25_spmd.clone.sunk | while | flops 886470 | bytes 335592 | solution.py:34
  668.4 72.6 %all-reduce.4 = f32[1536]{0:T(1024)S(1)} all-reduce(f32[1536]{0:T(1024)S(1)} %fusion.208), channel_id=1, replica_groups=mesh['tm'=8,'row'=32] {'row'}, use_global_device_ids=true, to_apply=%add.1 | all-reduce | flops 1536 | bytes 12288 | tf_op jit(solution)/shard_map/while
  744.8 73.1 %all-reduce.4 = f32[1536]{0:T(1024)S(1)} all-reduce(f32[1536]{0:T(1024)S(1)} %fusion.208), channel_id=1, replica_groups=mesh['tm'=8,'row'=32] {'row'}, use_global_device_ids=true, to_apply=%add.1 | all-reduce | flops 1536 | bytes 12288 | tf_op jit(solution)/shard_map/while
  821.7 70.6 %all-reduce.4 = f32[1536]{0:T(1024)S(1)} all-reduce(f32[1536]{0:T(1024)S(1)} %fusion.208), channel_id=1, replica_groups=mesh['tm'=8,'row'=32] {'row'}, use_global_device_ids=true, to_apply=%add.1 | all-reduce | flops 1536 | bytes 12288 | tf_op jit(solution)/shard_map/while
  896.2 72.7 %all-reduce.4 = f32[1536]{0:T(1024)S(1)} all-reduce(f32[1536]{0:T(1024)S(1)} %fusion.208), channel_id=1, replica_groups=mesh['tm'=8,'row'=32] {'row'}, use_global_device_ids=true, to_apply=%add.1 | all-reduce | flops 1536 | bytes 12288 | tf_op jit(solution)/shard_map/while
  972.7 70.6 %all-reduce.4 = f32[1536]{0:T(1024)S(1)} all-reduce(f32[1536]{0:T(1024)S(1)} %fusion.208), channel_id=1, replica_groups=mesh['tm'=8,'row'=32] {'row'}, use_global_device_ids=true, to_apply=%add.1 | all-reduce | flops 1536 | bytes 12288 | tf_op jit(solution)/shard_map/while
  1047.2 72.7 %all-reduce.4 = f32[1536]{0:T(1024)S(1)} all-reduce(f32[1536]{0:T(1024)S(1)} %fusion.208), channel_id=1, replica_groups=mesh['tm'=8,'row'=32] {'row'}, use_global_device_ids=true, to_apply=%add.1 | all-reduce | flops 1536 | bytes 12288 | tf_op jit(solution)/shard_map/while
  1123.8 70.7 %all-reduce.4 = f32[1536]{0:T(1024)S(1)} all-reduce(f32[1536]{0:T(1024)S(1)} %fusion.208), channel_id=1, replica_groups=mesh['tm'=8,'row'=32] {'row'}, use_global_device_ids=true, to_apply=%add.1 | all-reduce | flops 1536 | bytes 12288 | tf_op jit(solution)/shard_map/while
  1198.2 72.6 %all-reduce.4 = f32[1536]{0:T(1024)S(1)} all-reduce(f32[1536]{0:T(1024)S(1)} %fusion.208), channel_id=1, replica_groups=mesh['tm'=8,'row'=32] {'row'}, use_global_device_ids=true, to_apply=%add.1 | all-reduce | flops 1536 | bytes 12288 | tf_op jit(solution)/shard_map/while
  (261 shorter events, 101.8 us)
Async XLA Ops:
  7.2 88.6 %all-gather.2.cloned.1.call-start = ((), (), s32[]{:S(2)}) async-start(), calls=%async_computation | async-start | bytes 4866048 | tf_op jit(solution)/shard_map/all_gather | solution.py:20
  125.9 3.6 copy-start
  456.7 170.3 %copy-start.2 = (f32[1,48,1536]{2,1,0:T(8,128)S(1)}, f32[1,48,1536]{2,1,0:T(8,128)}, u32[]{:S(2)}) copy-start(f32[1,48,1536]{2,1,0:T(8,128)} %param.8) | copy-start | bytes 884740
  631.2 33.7 %copy-start.3 = (f32[1,48]{1,0:T(1,128)S(1)}, f32[1,48]{1,0:T(1,128)}, u32[]{:S(2)}) copy-start(f32[1,48]{1,0:T(1,128)} %param.9) | copy-start | bytes 580
  631.2 33.7 %copy-start.4 = (f32[48]{0:T(128)S(1)}, f32[48]{0:T(128)}, u32[]{:S(2)}) copy-start(f32[48]{0:T(128)} %param.11) | copy-start | bytes 580
  631.2 33.7 %copy-start.5 = (f32[1,48]{1,0:T(1,128)S(1)}, f32[1,48]{1,0:T(1,128)}, u32[]{:S(2)}) copy-start(f32[1,48]{1,0:T(1,128)} %param.10) | copy-start | bytes 580
  631.2 33.7 %copy-start.6 = (u32[256]{0:T(256)S(1)}, u32[256]{0:T(256)}, u32[]{:S(2)}) copy-start(u32[256]{0:T(256)} %constant.815) | copy-start | bytes 3076
  664.9 3.3 collective-permute-start
  741.4 3.3 collective-permute-start
  818.3 3.3 collective-permute-start
  892.8 3.3 collective-permute-start
  969.3 3.3 collective-permute-start
  1043.8 3.3 collective-permute-start
  1120.3 3.3 collective-permute-start
  1194.8 3.3 collective-permute-start
  1271.2 0.7 copy-start.1
  1271.3 0.7 copy-start.7
Sparse Core Ops, SparseCore 0:
  10.6 85.1 all-gather.1
where the time goes:
time: 1290 us; the launch traced here: 1280 us
  blocking collectives  576 us (45%)
  other arithmetic  407 us (32%)
  matrix products  89.3 us (7%)
  waiting for transfers between devices  88.5 us (7%)
  local copies, waits for them, and re-layouts  74.1 us (6%)
  between operations  23.1 us (2%)
  starting transfers between devices  15.4 us (1%)
    while x8, blocking collectives  576 us
    another operation x46, other arithmetic, per_device(): cholesky_factor = jnp.linalg.cholesky(whole_cov[0].astype(jnp.float32))  264 us
    another operation x3, other arithmetic, per_device(): gain = jax.scipy.linalg.cho_solve((cholesky_factor, True), cross[0].T).T  127 us
    all_gather x1, waiting for transfers between devices, per_device(): whole_cov = lax.all_gather(pred_cov, 'row', axis=1, tiled=True)  87.8 us
    another operation x22, matrix products, per_device(): cholesky_factor = jnp.linalg.cholesky(whole_cov[0].astype(jnp.float32))  50.1 us
    another operation x36, local copies, waits for them, and re-layouts  42.9 us
    another operation x46, matrix products, per_device(): gain = jax.scipy.linalg.cho_solve((cholesky_factor, True), cross[0].T).T  36.7 us
  transfers between devices with their start and end apart: 9, of which 1 were waited for; matrix products, arithmetic and copies ran while one was open for 0% of the time, Pallas kernels for 0%

commit v1 on v0

--- a/solution.py
+++ b/solution.py
@@ -17,7 +17,9 @@
 
 
 def per_device(pred_cov, cross, filt_mean, pred_mean, next_smoothed):
-    whole_cov = lax.all_gather(pred_cov, "row", axis=1, tiled=True)
+    whole_cov = jnp.concatenate(
+        lax.all_to_all(jnp.stack([pred_cov] * lax.axis_size("row")), "row", 0, 0), axis=1
+    )
     cholesky_factor = jnp.linalg.cholesky(whole_cov[0].astype(jnp.float32))
     gain = jax.scipy.linalg.cho_solve((cholesky_factor, True), cross[0].T).T
     steps = lax.axis_size("tm")

time: 1290 us -> 1300 us (level)
  waiting for transfers between devices: 88.5 us -> 108 us
  between operations: 23.1 us -> 9.72 us
    all_to_all x0 -> x1, waiting for transfers between devices: none -> 108 us  [per_device(): lax.all_to_all(jnp.stack([pred_cov] * lax.axis_size('row')), 'row', 0, 0)]
    all_gather x1 -> x0, waiting for transfers between devices: 87.8 us -> none  [per_device(): whole_cov = lax.all_gather(pred_cov, 'row', axis=1, tiled=True)]
    another operation x36 -> x37, local copies, waits for them, and re-layouts: 42.9 us -> 46.5 us
where the time goes in v1:
time: 1300 us; the launch traced here: 1290 us
  blocking collectives  573 us (44%)
  other arithmetic  407 us (31%)
  waiting for transfers between devices  108 us (8%)
  matrix products  89.1 us (7%)
  local copies, waits for them, and re-layouts  71.1 us (5%)
  starting transfers between devices  27.2 us (2%)
    while x8, blocking collectives  573 us
    another operation x46, other arithmetic, per_device(): cholesky_factor = jnp.linalg.cholesky(whole_cov[0].astype(jnp.float32))  264 us
    another operation x3, other arithmetic, per_device(): gain = jax.scipy.linalg.cho_solve((cholesky_factor, True), cross[0].T).T  127 us
    all_to_all x1, waiting for transfers between devices, per_device(): lax.all_to_all(jnp.stack([pred_cov] * lax.axis_size('row')), 'row', 0, 0)  108 us
    another operation x22, matrix products, per_device(): cholesky_factor = jnp.linalg.cholesky(whole_cov[0].astype(jnp.float32))  50.1 us
    another operation x36, local copies, waits for them, and re-layouts  42.9 us
    another operation x46, matrix products, per_device(): gain = jax.scipy.linalg.cho_solve((cholesky_factor, True), cross[0].T).T  36.5 us
  transfers between devices with their start and end apart: 9, of which 1 were waited for; matrix products, arithmetic and copies ran while one was open for 0% of the time, Pallas kernels for 0%

profile of v1, /device:TPU:12, one launch (start us, length us, event | category | flops | bytes accessed | tf_op | source)
XLA Modules:
  0.0 1291.4 jit_solution(10172952149628062248)
XLA Ops:
  0.6 3.6 stack.2
  4.2 11.7 all-to-all-start
  16.0 108.3 %all-to-all-done = bf16[32,1,48,1536]{3,2,1,0:T(8,128)(2,1)} async-done(((bf16[32,1,48,1536]{3,2,1,0:T(8,128)(2,1)}), bf16[32,1,48,1536]{3,2,1,0:T(8,128)(2,1)}, u32[]{:S(2)}, u32[]{:S(2)}) %all-to-all-start) | async-done | bytes 4718624 | tf_op jit(solution)/shard_map/all_to_all | solution.py:21
  124.3 7.3 bitcast_convert_fusion
  131.6 9.6 copy.11
  141.2 6.5 fusion.3
  147.7 3.6 copy-done
  151.4 11.7 cholesky.341
  163.1 9.8 custom-call.98
  172.9 4.8 cholesky.371
  177.8 2.8 constant_dynamic-update-slice_fusion.134
  182.4 12.0 cholesky.362
  195.1 9.8 custom-call.99
  209.3 11.7 cholesky.385
  222.3 9.8 custom-call.100
  233.8 3.3 convolution_subtract_fusion
  237.1 11.7 cholesky.715
  250.1 9.8 custom-call.101
  261.4 3.6 fusion.20
  265.0 11.9 cholesky.734
  278.2 9.8 custom-call.102
  289.4 3.8 fusion.23
  293.2 11.7 cholesky.754
  306.2 10.2 custom-call.103
  317.7 3.8 fusion.26
  321.5 11.7 cholesky.774
  334.5 9.8 custom-call.104
  345.5 3.8 fusion.29
  349.3 11.9 cholesky.794
  362.5 9.8 custom-call.105
  373.5 3.6 fusion.32
  377.0 11.7 cholesky.814
  390.1 10.2 custom-call.106
  401.4 3.3 fusion.35
  404.6 11.7 cholesky.834
  417.6 9.8 custom-call.107
  428.3 2.8 fusion.38
  431.2 11.9 cholesky.854
  444.4 9.8 custom-call.108
  457.3 11.7 cholesky.872
  478.6 8.5 select_select_fusion
  487.1 42.9 %while.12 = (s32[]{:T(128)}, f32[1536,1536]{1,0:T(8,128)}, s32[12,2]{0,1:T(2,128)S(1)}, f32[12,128,128]{2,1,0:T(8,128)}, s32[]{:T(128)}) while((s32[]{:T(128)}, f32[1536,1536]{1,0:T(8,128)}, s32[12,2]{0,1:T(2,128)S(1)}, f32[12,128,128]{2,1,0:T(8,128)}, s32[]{:T(128)}) %tuple.127), condition=%wide.while_cond, body=%wide.while_body.sunk | while | flops 2 | bytes 132705 | solution.py:24
  487.8 2.9 bitcast_dynamic-update-slice_fusion.2
  491.4 2.9 bitcast_dynamic-update-slice_fusion.2
  494.9 2.9 bitcast_dynamic-update-slice_fusion.2
  498.5 2.9 bitcast_dynamic-update-slice_fusion.2
  502.1 2.9 bitcast_dynamic-update-slice_fusion.2
  505.7 2.9 bitcast_dynamic-update-slice_fusion.2
  509.3 2.9 bitcast_dynamic-update-slice_fusion.2
  512.8 2.9 bitcast_dynamic-update-slice_fusion.2
  516.4 2.9 bitcast_dynamic-update-slice_fusion.2
  520.0 2.9 bitcast_dynamic-update-slice_fusion.2
  523.6 2.9 bitcast_dynamic-update-slice_fusion.2
  527.2 2.8 bitcast_dynamic-update-slice_fusion.2
  530.0 118.9 %custom-call.109 = f32[12,128,128]{1,2,0:T(8,128)S(1)} custom-call(f32[12,128,128]{2,1,0:T(8,128)} %get-tuple-element.47), custom_call_target="InvertDiagBlocksLowerTriangular" | custom-call | tf_op jit(solution)/shard_map/jit(_cho_solve)/triangular_solve | solution.py:24
  686.6 603.7 %while.13 = (s32[]{:T(128)}, f32[48]{0:T(128)S(1)}, pred[]{:T(512)}, f32[48]{0:T(128)S(1)}, f32[48]{0:T(128)S(1)}, /*index=5*/f32[48,1536]{1,0:T(8,128)S(1)}, f3...) while((s32[]{:T(128)}, f32[48]{0:T(128)S(1)}, ...), condition=%wide.region_25.26_spmd.clone, body=%wide.region_24.25_spmd.clone.sunk | while | flops 886470 | bytes 335592 | solution.py:36
  690.2 67.8 %all-reduce.4 = f32[1536]{0:T(1024)S(1)} all-reduce(f32[1536]{0:T(1024)S(1)} %fusion.208), channel_id=1, replica_groups=mesh['tm'=8,'row'=32] {'row'}, use_global_device_ids=true, to_apply=%add.1 | all-reduce | flops 1536 | bytes 12288 | tf_op jit(solution)/shard_map/while
  761.8 75.4 %all-reduce.4 = f32[1536]{0:T(1024)S(1)} all-reduce(f32[1536]{0:T(1024)S(1)} %fusion.208), channel_id=1, replica_groups=mesh['tm'=8,'row'=32] {'row'}, use_global_device_ids=true, to_apply=%add.1 | all-reduce | flops 1536 | bytes 12288 | tf_op jit(solution)/shard_map/while
  841.1 70.6 %all-reduce.4 = f32[1536]{0:T(1024)S(1)} all-reduce(f32[1536]{0:T(1024)S(1)} %fusion.208), channel_id=1, replica_groups=mesh['tm'=8,'row'=32] {'row'}, use_global_device_ids=true, to_apply=%add.1 | all-reduce | flops 1536 | bytes 12288 | tf_op jit(solution)/shard_map/while
  915.5 72.6 %all-reduce.4 = f32[1536]{0:T(1024)S(1)} all-reduce(f32[1536]{0:T(1024)S(1)} %fusion.208), channel_id=1, replica_groups=mesh['tm'=8,'row'=32] {'row'}, use_global_device_ids=true, to_apply=%add.1 | all-reduce | flops 1536 | bytes 12288 | tf_op jit(solution)/shard_map/while
  992.0 70.6 %all-reduce.4 = f32[1536]{0:T(1024)S(1)} all-reduce(f32[1536]{0:T(1024)S(1)} %fusion.208), channel_id=1, replica_groups=mesh['tm'=8,'row'=32] {'row'}, use_global_device_ids=true, to_apply=%add.1 | all-reduce | flops 1536 | bytes 12288 | tf_op jit(solution)/shard_map/while
  1066.4 72.6 %all-reduce.4 = f32[1536]{0:T(1024)S(1)} all-reduce(f32[1536]{0:T(1024)S(1)} %fusion.208), channel_id=1, replica_groups=mesh['tm'=8,'row'=32] {'row'}, use_global_device_ids=true, to_apply=%add.1 | all-reduce | flops 1536 | bytes 12288 | tf_op jit(solution)/shard_map/while
  1142.9 70.6 %all-reduce.4 = f32[1536]{0:T(1024)S(1)} all-reduce(f32[1536]{0:T(1024)S(1)} %fusion.208), channel_id=1, replica_groups=mesh['tm'=8,'row'=32] {'row'}, use_global_device_ids=true, to_apply=%add.1 | all-reduce | flops 1536 | bytes 12288 | tf_op jit(solution)/shard_map/while
  1217.3 72.6 %all-reduce.4 = f32[1536]{0:T(1024)S(1)} all-reduce(f32[1536]{0:T(1024)S(1)} %fusion.208), channel_id=1, replica_groups=mesh['tm'=8,'row'=32] {'row'}, use_global_device_ids=true, to_apply=%add.1 | all-reduce | flops 1536 | bytes 12288 | tf_op jit(solution)/shard_map/while
  (260 shorter events, 103.8 us)
Async XLA Ops:
  4.2 120.1 %all-to-all-start = ((bf16[32,1,48,1536]{3,2,1,0:T(8,128)(2,1)}), bf16[32,1,48,1536]{3,2,1,0:T(8,128)(2,1)}, u32[]{:S(2)}, u32[]{:S(2)}) async-start(bf16[32,1,48,1536]{3,2,1,0:T(8,128)(2,1)} %stack.2), calls=%async_computation | async-start | bytes 9437184 | tf_op jit(solution)/shard_map/all_to_all | solution.py:21
  147.7 3.6 copy-start
  478.6 170.3 %copy-start.2 = (f32[1,48,1536]{2,1,0:T(8,128)S(1)}, f32[1,48,1536]{2,1,0:T(8,128)}, u32[]{:S(2)}) copy-start(f32[1,48,1536]{2,1,0:T(8,128)} %param.8) | copy-start | bytes 884740
  653.0 33.5 %copy-start.3 = (f32[1,48]{1,0:T(1,128)S(1)}, f32[1,48]{1,0:T(1,128)}, u32[]{:S(2)}) copy-start(f32[1,48]{1,0:T(1,128)} %param.9) | copy-start | bytes 580
  653.1 33.5 %copy-start.4 = (f32[48]{0:T(128)S(1)}, f32[48]{0:T(128)}, u32[]{:S(2)}) copy-start(f32[48]{0:T(128)} %param.11) | copy-start | bytes 580
  653.1 33.5 %copy-start.5 = (f32[1,48]{1,0:T(1,128)S(1)}, f32[1,48]{1,0:T(1,128)}, u32[]{:S(2)}) copy-start(f32[1,48]{1,0:T(1,128)} %param.10) | copy-start | bytes 580
  653.1 33.5 %copy-start.6 = (u32[256]{0:T(256)S(1)}, u32[256]{0:T(256)}, u32[]{:S(2)}) copy-start(u32[256]{0:T(256)} %constant.815) | copy-start | bytes 3076
  686.6 3.4 collective-permute-start
  758.4 3.3 collective-permute-start
  837.6 3.3 collective-permute-start
  912.1 3.3 collective-permute-start
  988.5 3.3 collective-permute-start
  1063.0 3.3 collective-permute-start
  1139.4 3.3 collective-permute-start
  1213.9 3.3 collective-permute-start
  1290.3 0.7 copy-start.1
  1290.3 0.7 copy-start.7
